TPU v7x, 32 devices: a whole 2x2x4 slice. The times are simulated.
32 devices in a mesh: chan: 8 (over y, x, core), win: 4 (over z).
Axes of the slice: x: 2, y: 2, z: 4, core: 2. Of those that a mesh axis runs over, the one named last changes fastest.
Arguments:
- records: float32 [16, 1024, 256], P('win', 'chan'), may hold values from -180 to 180
- sources: int32 [32], replicated, may hold values from 0 to 255, as said below
Outputs:
- correlations: float32 [32, 256, 256], P('win', None, 'chan')
Inputs may be any that keep to these rules, and one draw needn't show every extreme that they name: `sources`: source s is one of the channels s * 8 to (s + 1) * 8 - 1; the first source is channel 0 and the last is channel 256 - 1.
All inputs are finite; a program needn't handle non-finite values.
Results may differ from a plain program's by a relative error of at most 0.00022.
Values sent between devices are 32-bit elements; how exact they have to be, the bound alone decides.
A program may use at most 64 MiB of HBM per device.

v0:
```python
import math
import jax
import jax.numpy as jnp
from jax import lax
from jax.sharding import PartitionSpec as P

HIGHEST = lax.Precision.HIGHEST
AMPLITUDE_FLOOR = 0.25
WHITE_EPSILON = 1e-06


def fourier_table(length):
    freq_count = length // 2
    freqs = jnp.arange(freq_count, dtype=jnp.int32)[:, None]
    sample_index = jnp.arange(length, dtype=jnp.int32)[None, :]
    angles = (freqs * sample_index % length).astype(jnp.float32) * (2.0 * math.pi / length)
    return jnp.concatenate([jnp.cos(angles), -jnp.sin(angles)], axis=0)


def band_table(freq_count, reach):
    rows_index = jnp.arange(freq_count, dtype=jnp.int32)[:, None]
    cols_index = jnp.arange(freq_count, dtype=jnp.int32)[None, :]
    return (jnp.abs(rows_index - cols_index) <= reach).astype(jnp.float32)


def inverse_table(length, lag_count, first_bin, bin_count, factor):
    freqs = first_bin + jnp.arange(bin_count, dtype=jnp.int32)
    lag_index = jnp.arange(lag_count, dtype=jnp.int32) - lag_count // 2
    angles = (lag_index[:, None] * freqs[None, :] % length).astype(jnp.float32) * (
        2.0 * math.pi / length
    )
    weights = jnp.where(freqs == 0, 1.0, 2.0).astype(jnp.float32)[None, :] * factor
    return jnp.concatenate([weights * jnp.cos(angles), -weights * jnp.sin(angles)], axis=1)


def running_level(padded, time_count, window_span):
    window_total = padded.shape[0]
    chans = padded.shape[2]
    running = jnp.concatenate(
        [jnp.zeros((window_total, 1, chans), jnp.float32), jnp.cumsum(jnp.abs(padded), axis=1)],
        axis=1,
    )
    return (running[:, window_span:] - running[:, :time_count]) / window_span


def local(records, sources):
    chan_count = lax.axis_size("chan")
    local_windows, local_time, all_channels = records.shape
    length = local_time * chan_count
    freq_count = length // 2
    chan_width = all_channels // chan_count
    half_width = min(16, local_time)
    smooth_reach = length // 32
    window_span = 2 * half_width + 1
    lag_count = length // 4
    forward = fourier_table(length)
    band_matrix = band_table(freq_count, smooth_reach)
    pieces = lax.all_to_all(records, "chan", split_axis=2, concat_axis=1, tiled=True)
    padded = jnp.pad(pieces, ((0, 0), (half_width, half_width), (0, 0)))
    amplitude = running_level(padded, length, window_span)
    whiten_pieces = pieces / jnp.maximum(amplitude, AMPLITUDE_FLOOR)
    spectrum = jnp.einsum("kt,wtc->wkc", forward, whiten_pieces, precision=HIGHEST)
    real_part = spectrum[:, :freq_count]
    imag_part = spectrum[:, freq_count:]
    magnitude = jnp.sqrt(real_part * real_part + imag_part * imag_part)
    smoothed = (
        jnp.einsum("jk,wkc->wjc", band_matrix, magnitude, precision=HIGHEST)
        / (2 * smooth_reach + 1)
        + WHITE_EPSILON
    )
    whitened = jnp.stack([real_part / smoothed, imag_part / smoothed], axis=1)
    band_data = lax.all_to_all(whitened, "win", split_axis=2, concat_axis=0, tiled=True)
    total_windows = band_data.shape[0]
    band_count = band_data.shape[2]
    source_count = sources.shape[0]
    chan_index = lax.axis_index("chan")
    channel_ids = jnp.arange(chan_width, dtype=jnp.int32)
    per_device = source_count // chan_count
    owned_local = (
        lax.dynamic_slice_in_dim(sources, chan_index * per_device, per_device)
        - chan_index * chan_width
    )
    selector = (owned_local[:, None] == channel_ids[None, :]).astype(jnp.float32)
    chosen = jnp.einsum("sc,wafc->wafs", selector, band_data, precision=HIGHEST)
    spectra = lax.all_gather(chosen, "chan", axis=3, tiled=True)
    source_real = spectra[:, 0]
    source_imag = spectra[:, 1]
    white_real = band_data[:, 0]
    white_imag = band_data[:, 1]
    cross_real = jnp.einsum(
        "wfs,wfc->fsc", source_real, white_real, precision=HIGHEST
    ) + jnp.einsum("wfs,wfc->fsc", source_imag, white_imag, precision=HIGHEST)
    cross_imag = jnp.einsum(
        "wfs,wfc->fsc", source_real, white_imag, precision=HIGHEST
    ) - jnp.einsum("wfs,wfc->fsc", source_imag, white_real, precision=HIGHEST)
    stacked = jnp.stack([cross_real, cross_imag])
    factor = 1.0 / math.sqrt(total_windows * freq_count)
    band_start = lax.axis_index("win") * band_count
    band_table_part = inverse_table(length, lag_count, band_start, band_count, factor).reshape(
        lag_count, 2, band_count
    )
    return lax.psum_scatter(
        jnp.einsum("tak,aksc->stc", band_table_part, stacked, precision=HIGHEST),
        "win",
        scatter_dimension=0,
        tiled=True,
    )


def solution(mesh):
    placed = (P("win", "chan", None), P())
    return jax.shard_map(
        local, mesh=mesh, in_specs=placed, out_specs=P("win", None, "chan"), check_vma=False
    )
```

profile of v0, /device:TPU:0, one launch (start us, length us, event | category | flops | bytes accessed | tf_op | source)
XLA Modules:
  0.0 168.4 jit_solution(1420910097086612107)
XLA Ops:
  6.5 2.1 %copy.58 = f32[4,128,256]{1,0,2:T(4,128)} copy(f32[4,128,256]{2,1,0:T(8,128)} %param.2) | data formatting | bytes 1048576 | tf_op args[0]
  8.6 5.2 %all-to-all-start = ((f32[4,128,256]{1,0,2:T(4,128)}), f32[4,128,256]{1,0,2:T(4,128)S(1)}, u32[]{:S(2)}, u32[]{:S(2)}) async-start(f32[4,128,256]{1,0,2:T(4,128)} %copy.58), calls=%async_computation | async-start | bytes 1048576 | tf_op jit(solution)/shard_map/all_to_all | solution.py:58
  13.8 9.2 %sine_negate_fusion = (f32[512,1024]{1,0:T(8,128)}, f32[512,1024]{1,0:T(8,128)}) fusion(), kind=kLoop, calls=%fused_computation.15 | loop fusion | flops 7864320 | bytes 4194304 | tf_op jit(solution)/shard_map/neg | solution.py:17
  23.0 0.5 all-to-all-done
  23.6 0.2 abs_bitcast_fusion
  23.9 0.1 reshape.194
  24.0 36.3 %reduce-window.6 = f32[4,32,9,128]{3,2,1,0:T(8,128)S(1)} reduce-window(f32[4,32,9,128]{3,2,1,0:T(8,128)S(1)} %reshape.194, f32[]{:T(128)} %constant.22.clone.1), window={size=1x1x1x128 pad=0_0x0_0x0_0x127_0}, to_apply=%region_0.1 | reduce-window | flops 18726912 | bytes 1179652 | tf_op jit(solution)/shard_map/reduce-window
  60.3 0.3 slice.45
  60.6 0.4 copy.61
  61.0 0.1 copy.62
  61.1 0.3 broadcast_add_fusion
  61.4 0.1 reduce_window_sum.16
  61.5 6.6 %fusion.14 = f32[4,1024,32]{1,2,0:T(8,128)S(1)} fusion(f32[512,1024]{1,0:T(8,128)} %get-tuple-element.13, f32[512,1024]{1,0:T(8,128)} %get-tuple-element.14, f32[4,1056,32]{1,2,0:T(8,128)S(1)} %bitcast.87, f32[4,1152,32]{1,2,0:T(8,128)S(1)} %bitcast.86, f32[4,8,4,8,128]{4,3,2,1,0:T(8,128)S(1)} %bitcast.84), kind=kOutput, calls=%fused_computation.20 | convolution fusion | flops 1612185600 | bytes 6356992 | tf_op jit(solution)/shard_map/kt,wtc->wkc/dot_general | solution.py:62
  68.1 0.7 divide_bitcast_fusion.1
  68.9 1.1 copy.63
  69.9 0.0 copy-start.2
  70.0 2.1 %reshape.201 = f32[4,1,32768]{2,1,0:T(1,128)} reshape(f32[512,2,4,32]{3,2,1,0:T(4,128)S(1)} %bitcast.79) | data formatting | bytes 1048576
  72.0 4.9 %all-to-all-start.1 = ((f32[4,1,32768]{2,1,0:T(1,128)}), f32[4,1,32768]{2,1,0:T(1,128)S(1)}, u32[]{:S(2)}, u32[]{:S(2)}) async-start(f32[4,1,32768]{2,1,0:T(1,128)} %reshape.201), calls=%async_computation.1 | async-start | bytes 1048576 | tf_op jit(solution)/shard_map/all_to_all | solution.py:72
  76.9 0.0 reduce-scatter.2.cloned.1.call-start
  76.9 0.0 copy-done.2
  76.9 0.1 dynamic-slice_subtract_fusion
  77.0 1.3 cosine_multiply_fusion
  78.2 13.3 %all-to-all-done.1 = f32[4,1,32768]{2,1,0:T(1,128)S(1)} async-done(((f32[4,1,32768]{2,1,0:T(1,128)}), f32[4,1,32768]{2,1,0:T(1,128)S(1)}, u32[]{:S(2)}, u32[]{:S(2)}) %all-to-all-start.1) | async-done | bytes 524320 | tf_op jit(solution)/shard_map/all_to_all | solution.py:72
  91.5 0.5 broadcast.245
  92.0 2.1 %reduce = f32[4,32768]{1,0:T(4,128)S(1)} reduce(f32[4,1,32768]{2,1,0:T(1,128)S(1)} %all-to-all-done.1, f32[]{:T(128)} %broadcast.245), dimensions={1}, to_apply=%all_to_all.30.reduce_sub_computation | reduce | bytes 1048580 | tf_op jit(solution)/shard_map/all_to_all | solution.py:72
  94.2 1.1 reshape.202
  95.3 0.8 copy.64
  96.2 0.3 fusion.49
  96.5 10.0 %all_gather.3 = f32[16,2,128,32]{2,0,1,3:T(8,128)S(1)} all-gather(f32[16,2,128,4]{2,0,1,3:T(8,128)S(1)} %copy.65), channel_id=1, replica_groups=mesh['chan'=8,'win'=4] {'chan'}, dimensions={3}, use_global_device_ids=true | all-gather | bytes 589824 | tf_op jit(solution)/shard_map/all_gather | solution.py:85
  106.5 0.7 fusion.60
  107.2 0.5 copy.77
  107.7 0.5 copy.67
  108.2 1.5 copy.78
  109.7 1.4 copy.69
  111.1 0.0 copy-start
  111.1 3.6 %fusion.21 = f32[128,32,32]{2,1,0:T(8,128)S(1)} fusion(f32[16,128,32]{2,0,1:T(8,128)S(1)} %copy.67, f32[16,1,128,32]{3,0,2,1:T(8,128)S(1)} %copy.77), kind=kOutput, calls=%fused_computation.28 | convolution fusion | flops 25165824 | bytes 1048576 | tf_op jit(solution)/shard_map/wfs,wfc->fsc/dot_general | solution.py:90
  114.7 0.0 copy-done
  114.7 3.6 %fusion.19 = f32[128,32,32]{2,1,0:T(8,128)S(1)} fusion(f32[16,128,32]{2,0,1:T(8,128)S(1)} %copy-done, f32[16,1,128,32]{3,0,2,1:T(8,128)S(1)} %copy.77), kind=kOutput, calls=%fused_computation.26 | convolution fusion | flops 25165824 | bytes 1048576 | tf_op jit(solution)/shard_map/wfs,wfc->fsc/dot_general | solution.py:93
  118.4 3.9 %add_bitcast_fusion = f32[1,128,32,32]{3,2,1,0:T(8,128)S(1)} fusion(f32[128,32,32]{2,1,0:T(8,128)S(1)} %fusion.21, f32[16,128,32]{2,0,1:T(8,128)S(1)} %copy-done, f32[16,1,128,32]{3,0,2,1:T(8,128)S(1)} %copy.78), kind=kOutput, calls=%fused_computation.14 | convolution fusion | flops 25296896 | bytes 1572864 | tf_op jit(solution)/shard_map/wfs,wfc->fsc/dot_general | solution.py:92
  122.3 3.7 %subtract_bitcast_fusion = f32[1,128,32,32]{3,2,1,0:T(8,128)S(1)} fusion(f32[128,32,32]{2,1,0:T(8,128)S(1)} %fusion.19, f32[16,128,32]{2,0,1:T(8,128)S(1)} %copy.67, f32[16,1,128,32]{3,0,2,1:T(8,128)S(1)} %copy.78), kind=kOutput, calls=%fused_computation.13 | convolution fusion | flops 25296896 | bytes 1572864 | tf_op jit(solution)/shard_map/wfs,wfc->fsc/dot_general | solution.py:95
  126.0 0.0 copy-start.1
  126.0 0.6 pad_maximum_fusion
  126.6 0.3 copy-done.1
  126.9 9.1 %fusion.11 = f32[32,256,32]{1,2,0:T(8,128)} fusion(f32[2,128,32,32]{3,2,1,0:T(8,128)S(1)} %pad_maximum_fusion, f32[256,1,128]{2,0,1:T(8,128)S(1)} %copy-done.1, f32[256,1,128]{2,0,1:T(8,128)S(1)} %get-tuple-element.11), kind=kOutput, calls=%fused_computation.19 | convolution fusion | flops 805371904 | bytes 2359296 | tf_op jit(solution)/shard_map/tak,aksc->stc/dot_general | solution.py:103
  136.0 0.0 reduce-scatter.2.cloned.1.call-update
  136.0 25.6 %reduce-scatter.2.cloned.1.call-done = f32[8,256,32]{1,2,0:T(8,128)} async-done(((f32[32,256,32]{1,2,0:T(8,128)}), f32[8,256,32]{1,2,0:T(8,128)}) %reduce-scatter.2.cloned.1.call-update) | async-done | bytes 262160 | tf_op jit(solution)/shard_map/reduce_scatter | solution.py:102
  (11 shorter events, 0.2 us)
Async XLA Ops:
  8.6 14.9 %all-to-all-start = ((f32[4,128,256]{1,0,2:T(4,128)}), f32[4,128,256]{1,0,2:T(4,128)S(1)}, u32[]{:S(2)}, u32[]{:S(2)}) async-start(f32[4,128,256]{1,0,2:T(4,128)} %copy.58), calls=%async_computation | async-start | bytes 1048576 | tf_op jit(solution)/shard_map/all_to_all | solution.py:58
  69.9 6.9 %copy-start.2 = (s32[32]{0:T(128)S(1)}, s32[32]{0:T(128)}, u32[]{:S(2)}) copy-start(s32[32]{0:T(128)} %param.3) | copy-start | bytes 388
  72.0 19.5 %all-to-all-start.1 = ((f32[4,1,32768]{2,1,0:T(1,128)}), f32[4,1,32768]{2,1,0:T(1,128)S(1)}, u32[]{:S(2)}, u32[]{:S(2)}) async-start(f32[4,1,32768]{2,1,0:T(1,128)} %reshape.201), calls=%async_computation.1 | async-start | bytes 1048576 | tf_op jit(solution)/shard_map/all_to_all | solution.py:72
  76.9 84.7 %reduce-scatter.2.cloned.1.call-start = ((), (), s32[]{:S(2)}) async-start(), calls=%async_computation.3 | async-start | bytes 1310720 | tf_op jit(solution)/shard_map/reduce_scatter | solution.py:102
  111.1 3.6 %copy-start = (f32[16,128,32]{2,0,1:T(8,128)S(1)}, f32[16,128,32]{2,0,1:T(8,128)}, u32[]{:S(2)}) copy-start(f32[16,128,32]{2,0,1:T(8,128)} %copy.69) | copy-start | bytes 786436
  126.0 0.9 copy-start.1
Sparse Core Ops, SparseCore 0:
  136.1 25.3 reduce-scatter.1
where the time goes:
time: 169 us; the launch traced here: 168 us
  other arithmetic  50.1 us (30%)
  waiting for transfers between devices  39.4 us (23%)
  matrix products  31.5 us (19%)
  local copies, waits for them, and re-layouts  13.8 us (8%)
  between operations  13.6 us (8%)
  starting transfers between devices  10.1 us (6%)
  blocking collectives  9.97 us (6%)
    another operation x3, other arithmetic  36.6 us
    reduce_scatter x1, waiting for transfers between devices, local(): lax.psum_scatter(jnp.einsum('tak,aksc->stc', band_table_part, stacked, pr...  25.6 us
    all_to_all x1, waiting for transfers between devices, local(): lax.all_to_all(whitened, 'win', split_axis=2, concat_axis=0, tiled=True)  13.3 us
    all_gather x1, blocking collectives, local(): spectra = lax.all_gather(chosen, 'chan', axis=3, tiled=True)  9.97 us
    neg x1, other arithmetic, fourier_table(): return jnp.concatenate([jnp.cos(angles), -jnp.sin(angles)], axis=0)  9.19 us
    dot_general x1, matrix products, local(): jnp.einsum('tak,aksc->stc', band_table_part, stacked, precision=HIGHEST)  9.09 us
    unnamed x11, local copies, waits for them, and re-layouts  7.61 us
    dot_general x1, matrix products, local(): jnp.einsum('kt,wtc->wkc', forward, whiten_pieces, precision=HIGHEST)  6.57 us
  transfers between devices with their start and end apart: 3, of which 3 were waited for; matrix products, arithmetic and copies ran while one was open for 6% of the time, Pallas kernels for 0%

commit v1 on v0

--- a/solution.py
+++ b/solution.py
@@ -69,7 +69,10 @@
         + WHITE_EPSILON
     )
     whitened = jnp.stack([real_part / smoothed, imag_part / smoothed], axis=1)
-    band_data = lax.all_to_all(whitened, "win", split_axis=2, concat_axis=0, tiled=True)
+    band_data = jnp.concatenate(
+        lax.all_to_all(jnp.stack(jnp.split(whitened, lax.axis_size("win"), axis=2)), "win", 0, 0),
+        axis=0,
+    )
     total_windows = band_data.shape[0]
     band_count = band_data.shape[2]
     source_count = sources.shape[0]

time: 169 us -> 162 us (0.959)
  local copies, waits for them, and re-layouts: 13.8 us -> 8.23 us
    all_to_all x1 -> x0, other arithmetic: 2.14 us -> none  [local(): lax.all_to_all(whitened, 'win', split_axis=2, concat_axis=0, tiled=True)]
    squeeze x3 -> x0, local copies, waits for them, and re-layouts: 1.9 us -> none  [the longest x1 1.36 us: local(): white_imag = band_data[:, 1]]
    another operation x4 -> x5, other arithmetic: 36.7 us -> 37.5 us
  transfers between devices with their start and end apart: 3 -> 3, of which waited for: 3 -> 3; matrix products, arithmetic and copies ran while one was open for 6% -> 7% of each run, Pallas kernels for 0% -> 0%
where the time goes in v1:
time: 162 us
  other arithmetic  48.8 us (30%)
  waiting for transfers between devices  39.4 us (24%)
  matrix products  31.5 us (19%)
  between operations  13.6 us (8%)
  blocking collectives  10.2 us (6%)
  starting transfers between devices  10.1 us (6%)
  local copies, waits for them, and re-layouts  8.23 us (5%)
    another operation x3, other arithmetic  36.6 us
    reduce_scatter x1, waiting for transfers between devices, local(): lax.psum_scatter(jnp.einsum('tak,aksc->stc', band_table_part, stacked, pr...  25.6 us
    all_to_all x1, waiting for transfers between devices, local(): lax.all_to_all(jnp.stack(jnp.split(whitened, lax.axis_size('win'), axis=2...  13.2 us
    all_gather x1, blocking collectives, local(): spectra = lax.all_gather(chosen, 'chan', axis=3, tiled=True)  10.2 us
    neg x1, other arithmetic, fourier_table(): return jnp.concatenate([jnp.cos(angles), -jnp.sin(angles)], axis=0)  9.17 us
    dot_general x1, matrix products, local(): jnp.einsum('tak,aksc->stc', band_table_part, stacked, precision=HIGHEST)  9.09 us
    dot_general x1, matrix products, local(): jnp.einsum('kt,wtc->wkc', forward, whiten_pieces, precision=HIGHEST)  6.57 us
    unnamed x11, local copies, waits for them, and re-layouts  6.26 us
  transfers between devices with their start and end apart: 3, of which 3 were waited for; matrix products, arithmetic and copies ran while one was open for 7% of the time, Pallas kernels for 0%

profile of v1, /device:TPU:0, one launch (start us, length us, event | category | flops | bytes accessed | tf_op | source)
XLA Modules:
  0.0 161.8 jit_solution(16420873942070988072)
XLA Ops:
  6.5 2.1 %copy.50 = f32[4,128,256]{1,0,2:T(4,128)} copy(f32[4,128,256]{2,1,0:T(8,128)} %param.2) | data formatting | bytes 1048576 | tf_op args[0]
  8.6 5.2 %all-to-all-start = ((f32[4,128,256]{1,0,2:T(4,128)}), f32[4,128,256]{1,0,2:T(4,128)S(1)}, u32[]{:S(2)}, u32[]{:S(2)}) async-start(f32[4,128,256]{1,0,2:T(4,128)} %copy.50), calls=%async_computation | async-start | bytes 1048576 | tf_op jit(solution)/shard_map/all_to_all | solution.py:58
  13.8 9.2 %sine_negate_fusion = (f32[512,1024]{1,0:T(8,128)}, f32[512,1024]{1,0:T(8,128)}) fusion(), kind=kLoop, calls=%fused_computation.15 | loop fusion | flops 7864320 | bytes 4194304 | tf_op jit(solution)/shard_map/neg | solution.py:17
  23.0 0.5 all-to-all-done
  23.6 0.2 abs_bitcast_fusion
  23.9 0.1 reshape.197
  24.0 36.3 %reduce-window.6 = f32[4,32,9,128]{3,2,1,0:T(8,128)S(1)} reduce-window(f32[4,32,9,128]{3,2,1,0:T(8,128)S(1)} %reshape.197, f32[]{:T(128)} %constant.22.clone.1), window={size=1x1x1x128 pad=0_0x0_0x0_0x127_0}, to_apply=%region_0.1 | reduce-window | flops 18726912 | bytes 1179652 | tf_op jit(solution)/shard_map/reduce-window
  60.2 0.3 slice.45
  60.6 0.4 copy.53
  61.0 0.1 copy.54
  61.1 0.3 broadcast_add_fusion
  61.4 0.1 reduce_window_sum.16
  61.5 6.6 %fusion.14 = f32[4,1024,32]{1,2,0:T(8,128)S(1)} fusion(f32[512,1024]{1,0:T(8,128)} %get-tuple-element.17, f32[512,1024]{1,0:T(8,128)} %get-tuple-element.18, f32[4,1056,32]{1,2,0:T(8,128)S(1)} %bitcast.90, f32[4,1152,32]{1,2,0:T(8,128)S(1)} %bitcast.89, f32[4,8,4,8,128]{4,3,2,1,0:T(8,128)S(1)} %bitcast.87), kind=kOutput, calls=%fused_computation.20 | convolution fusion | flops 1612185600 | bytes 6356992 | tf_op jit(solution)/shard_map/kt,wtc->wkc/dot_general | solution.py:62
  68.1 0.7 divide_bitcast_fusion.1
  68.8 0.0 copy-start.2
  68.8 0.1 fusion.53
  68.9 0.9 pad_maximum_fusion.1
  69.7 4.9 %all-to-all-start.1 = ((f32[4,4,2,128,32]{3,4,1,2,0:T(8,128)}), f32[4,4,2,128,32]{3,4,1,2,0:T(8,128)S(1)}, u32[]{:S(2)}, u32[]{:S(2)}) async-start(f32[4,4,2,128,32]{3,4,1,2,0:T(8,128)} %pad_maximum_fusion.1), calls=%async_computation.1 | async-start | bytes 1048576 | tf_op jit(solution)/shard_map/all_to_all | solution.py:73
  74.6 0.0 reduce-scatter.2.cloned.1.call-start
  74.6 0.0 copy-done.2
  74.6 0.1 dynamic-slice_subtract_fusion
  74.7 1.3 cosine_multiply_fusion
  76.0 13.2 %all-to-all-done.1 = f32[4,4,2,128,32]{3,4,1,2,0:T(8,128)S(1)} async-done(((f32[4,4,2,128,32]{3,4,1,2,0:T(8,128)}), f32[4,4,2,128,32]{3,4,1,2,0:T(8,128)S(1)}, u32[]{:S(2)}, u32[]{:S(2)}) %all-to-all-start.1) | async-done | bytes 524320 | tf_op jit(solution)/shard_map/all_to_all | solution.py:73
  89.3 0.3 fusion.60
  89.6 10.2 %all_gather.3 = f32[16,2,128,32]{2,0,1,3:T(8,128)S(1)} all-gather(f32[16,2,128,4]{2,0,1,3:T(8,128)S(1)} %copy.56), channel_id=1, replica_groups=mesh['chan'=8,'win'=4] {'chan'}, dimensions={3}, use_global_device_ids=true | all-gather | bytes 589824 | tf_op jit(solution)/shard_map/all_gather | solution.py:88
  99.8 0.7 fusion.72
  100.5 0.5 copy.66
  101.1 0.5 copy.67
  101.6 1.5 copy.68
  103.1 1.4 copy.69
  104.4 0.0 copy-start
  104.4 3.6 %fusion.23 = f32[128,32,32]{2,1,0:T(8,128)S(1)} fusion(f32[16,1,128,32]{3,0,2,1:T(8,128)S(1)} %copy.67, f32[16,1,128,32]{3,0,2,1:T(8,128)S(1)} %copy.66), kind=kOutput, calls=%fused_computation.30 | convolution fusion | flops 25165824 | bytes 1048576 | tf_op jit(solution)/shard_map/wfs,wfc->fsc/dot_general | solution.py:93
  108.1 0.0 copy-done
  108.1 3.6 %fusion.17 = f32[128,32,32]{2,1,0:T(8,128)S(1)} fusion(f32[16,1,128,32]{3,0,2,1:T(8,128)S(1)} %copy-done, f32[16,1,128,32]{3,0,2,1:T(8,128)S(1)} %copy.66), kind=kOutput, calls=%fused_computation.24 | convolution fusion | flops 25165824 | bytes 1048576 | tf_op jit(solution)/shard_map/wfs,wfc->fsc/dot_general | solution.py:96
  111.7 3.9 %add_bitcast_fusion = f32[1,128,32,32]{3,2,1,0:T(8,128)S(1)} fusion(f32[128,32,32]{2,1,0:T(8,128)S(1)} %fusion.23, f32[16,1,128,32]{3,0,2,1:T(8,128)S(1)} %copy-done, f32[16,1,128,32]{3,0,2,1:T(8,128)S(1)} %copy.68), kind=kOutput, calls=%fused_computation.14 | convolution fusion | flops 25296896 | bytes 1572864 | tf_op jit(solution)/shard_map/wfs,wfc->fsc/dot_general | solution.py:95
  115.6 3.7 %subtract_bitcast_fusion = f32[1,128,32,32]{3,2,1,0:T(8,128)S(1)} fusion(f32[128,32,32]{2,1,0:T(8,128)S(1)} %fusion.17, f32[16,1,128,32]{3,0,2,1:T(8,128)S(1)} %copy.68, f32[16,1,128,32]{3,0,2,1:T(8,128)S(1)} %copy.67), kind=kOutput, calls=%fused_computation.13 | convolution fusion | flops 25296896 | bytes 1572864 | tf_op jit(solution)/shard_map/wfs,wfc->fsc/dot_general | solution.py:98
  119.3 0.0 copy-start.1
  119.3 0.6 pad_maximum_fusion
  119.9 0.3 copy-done.1
  120.2 9.1 %fusion.11 = f32[32,256,32]{1,2,0:T(8,128)} fusion(f32[2,128,32,32]{3,2,1,0:T(8,128)S(1)} %pad_maximum_fusion, f32[256,1,128]{2,0,1:T(8,128)S(1)} %copy-done.1, f32[256,1,128]{2,0,1:T(8,128)S(1)} %get-tuple-element.15), kind=kOutput, calls=%fused_computation.19 | convolution fusion | flops 805371904 | bytes 2359296 | tf_op jit(solution)/shard_map/tak,aksc->stc/dot_general | solution.py:106
  129.3 0.0 reduce-scatter.2.cloned.1.call-update
  129.4 25.6 %reduce-scatter.2.cloned.1.call-done = f32[8,256,32]{1,2,0:T(8,128)} async-done(((f32[32,256,32]{1,2,0:T(8,128)}), f32[8,256,32]{1,2,0:T(8,128)}) %reduce-scatter.2.cloned.1.call-update) | async-done | bytes 262160 | tf_op jit(solution)/shard_map/reduce_scatter | solution.py:105
  (11 shorter events, 0.2 us)
Async XLA Ops:
  8.6 14.9 %all-to-all-start = ((f32[4,128,256]{1,0,2:T(4,128)}), f32[4,128,256]{1,0,2:T(4,128)S(1)}, u32[]{:S(2)}, u32[]{:S(2)}) async-start(f32[4,128,256]{1,0,2:T(4,128)} %copy.50), calls=%async_computation | async-start | bytes 1048576 | tf_op jit(solution)/shard_map/all_to_all | solution.py:58
  68.8 5.8 %copy-start.2 = (s32[32]{0:T(128)S(1)}, s32[32]{0:T(128)}, u32[]{:S(2)}) copy-start(s32[32]{0:T(128)} %param.3) | copy-start | bytes 388
  69.7 19.5 %all-to-all-start.1 = ((f32[4,4,2,128,32]{3,4,1,2,0:T(8,128)}), f32[4,4,2,128,32]{3,4,1,2,0:T(8,128)S(1)}, u32[]{:S(2)}, u32[]{:S(2)}) async-start(f32[4,4,2,128,32]{3,4,1,2,0:T(8,128)} %pad_maximum_fusion.1), calls=%async_computation.1 | async-start | bytes 1048576 | tf_op jit(solution)/shard_map/all_to_all | solution.py:73
  74.6 80.3 %reduce-scatter.2.cloned.1.call-start = ((), (), s32[]{:S(2)}) async-start(), calls=%async_computation.3 | async-start | bytes 1310720 | tf_op jit(solution)/shard_map/reduce_scatter | solution.py:105
  104.4 3.6 %copy-start = (f32[16,1,128,32]{3,0,2,1:T(8,128)S(1)}, f32[16,1,128,32]{3,0,2,1:T(8,128)}, u32[]{:S(2)}) copy-start(f32[16,1,128,32]{3,0,2,1:T(8,128)} %copy.69) | copy-start | bytes 786436
  119.3 0.9 copy-start.1
Sparse Core Ops, SparseCore 0:
  129.5 25.4 reduce-scatter.1
